TPU v7x, 32 devices: a whole 2x2x4 slice. The times are simulated.
32 devices in a mesh: cuts: 2 (over x), frame: 8 (over z, y), coil: 2 (over core).
Axes of the slice: x: 2, y: 2, z: 4, core: 2. Of those that a mesh axis runs over, the one named last changes fastest.
Arguments:
- spatial: bfloat16 [512, 32, 512], P(('cuts', 'coil', 'frame')), parts along dimension 0, may hold values from -6 to 6
- temporal: bfloat16 [32, 64], P(('cuts', 'frame')), parts along dimension 0, may hold values from -0.75 to 0.75
- kspace: bfloat16 [32, 32, 256, 512], P(('cuts', 'frame'), 'coil'), parts along dimension 0, may hold values from -2 to 2
- sampled: int32 [32, 256], P(('cuts', 'frame')), parts along dimension 0, may hold values 0 or 1
- sensitivity: bfloat16 [64, 256, 512], P(('cuts', 'coil')), parts along dimension 0, may hold values from -1 to 1
Outputs:
- spatial_grad: float32 [512, 32, 512], P(('cuts', 'coil', 'frame')), parts along dimension 0
- temporal_grad: float32 [32, 64], P(('cuts', 'frame')), parts along dimension 0
There are 2 independent parts, one for each index of `cuts`. A program takes and returns all parts, laid end to end along the dimension named above; each array names one. Nothing has to cross between parts.
All inputs are finite; a program needn't handle non-finite values. No bound on the sum of `sampled` on one device may be relied on, other than what follows from the above.
Results may differ from a plain program's by a relative error of at most 0.003.
Values may be sent and summed in bfloat16 or wider, within the bound.
No kernel may reach another device: no remote copies, remote signals or barrier semaphores. Data moves between devices by JAX's collectives and lax.ppermute only.
A program may use at most 128 MiB of HBM per device.

v0:
```python
import math
import jax
import jax.numpy as jnp
from jax import lax
from jax.sharding import PartitionSpec as P


def split_parts(values):
    half_width = values.shape[-1] // 2
    return (values[..., :half_width], values[..., half_width:])


def dft_block(length):
    index = jnp.arange(length, dtype=jnp.int32)
    angles = (index[:, None] * index[None, :] % length).astype(jnp.float32) * (
        2.0 * math.pi / length
    )
    norm_factor = 1.0 / math.sqrt(length)
    cosine = jnp.cos(angles) * norm_factor
    sine_part = -jnp.sin(angles) * norm_factor
    upper_rows = jnp.concatenate([cosine, sine_part], 1)
    lower_rows = jnp.concatenate([-sine_part, cosine], 1)
    return jnp.concatenate([upper_rows, lower_rows], 0).astype(jnp.bfloat16)


def to_image(temporal, spatial):
    temp_real, temp_imag = split_parts(temporal)
    spat_real, spat_imag = split_parts(spatial)
    image_real = jnp.einsum(
        "tr,xry->txy", temp_real, spat_real, preferred_element_type=jnp.float32
    ) - jnp.einsum("tr,xry->txy", temp_imag, spat_imag, preferred_element_type=jnp.float32)
    image_imag = jnp.einsum(
        "tr,xry->txy", temp_real, spat_imag, preferred_element_type=jnp.float32
    ) + jnp.einsum("tr,xry->txy", temp_imag, spat_real, preferred_element_type=jnp.float32)
    return jnp.concatenate([image_real, image_imag], -1).astype(jnp.bfloat16)


def factor_grad(temporal, grad_image):
    temp_real, temp_imag = split_parts(temporal)
    grad_real, grad_imag = split_parts(grad_image)
    spatial_real = jnp.einsum(
        "tr,txy->xry", temp_real, grad_real, preferred_element_type=jnp.float32
    ) + jnp.einsum("tr,txy->xry", temp_imag, grad_imag, preferred_element_type=jnp.float32)
    spatial_imag = jnp.einsum(
        "tr,txy->xry", temp_real, grad_imag, preferred_element_type=jnp.float32
    ) - jnp.einsum("tr,txy->xry", temp_imag, grad_real, preferred_element_type=jnp.float32)
    return jnp.concatenate([spatial_real, spatial_imag], -1)


def frame_grad(spatial, grad_image):
    spat_real, spat_imag = split_parts(spatial)
    grad_real, grad_imag = split_parts(grad_image)
    temporal_real = jnp.einsum(
        "xry,txy->tr", spat_real, grad_real, preferred_element_type=jnp.float32
    ) + jnp.einsum("xry,txy->tr", spat_imag, grad_imag, preferred_element_type=jnp.float32)
    temporal_imag = jnp.einsum(
        "xry,txy->tr", spat_real, grad_imag, preferred_element_type=jnp.float32
    ) - jnp.einsum("xry,txy->tr", spat_imag, grad_real, preferred_element_type=jnp.float32)
    return jnp.concatenate([temporal_real, temporal_imag], -1)


def coil_adjoint(image, measured, sampled_row, sensitivity, block):
    image_real, image_imag = split_parts(image.astype(jnp.float32))
    sens_real, sens_imag = split_parts(sensitivity.astype(jnp.float32))
    coil_real = sens_real * image_real[None] - sens_imag * image_imag[None]
    coil_imag = sens_real * image_imag[None] + sens_imag * image_real[None]
    coil_image = jnp.concatenate([coil_real, coil_imag], -1).astype(jnp.bfloat16)
    coil_count, row_count, full_width = coil_image.shape
    spectrum = jnp.dot(
        coil_image.reshape(coil_count * row_count, full_width),
        block,
        preferred_element_type=jnp.float32,
    ).reshape(coil_count, row_count, full_width)
    line_keep = jnp.concatenate([sampled_row, sampled_row]).astype(jnp.float32)
    misfit = (line_keep * (spectrum - measured.astype(jnp.float32))).astype(jnp.bfloat16)
    adjoint = jnp.dot(
        misfit.reshape(coil_count * row_count, full_width),
        block.T,
        preferred_element_type=jnp.float32,
    ).reshape(coil_count, row_count, full_width)
    back_real, back_imag = split_parts(adjoint)
    grad_real = jnp.sum(sens_real * back_real + sens_imag * back_imag, axis=0)
    grad_imag = jnp.sum(sens_real * back_imag - sens_imag * back_real, axis=0)
    return jnp.concatenate([grad_real, grad_imag], -1)


def on_device(spatial, temporal, kspace, sampled, sensitivity):
    block = dft_block(spatial.shape[2] // 2)
    temporal_all = lax.all_gather(temporal, "frame", axis=0, tiled=True)
    image_rows = to_image(temporal_all, spatial)
    image_half = lax.all_to_all(image_rows, "frame", split_axis=0, concat_axis=1, tiled=True)
    image_full = lax.all_gather(image_half, "coil", axis=1, tiled=True)
    coil_partial = lax.map(
        lambda frame_item: coil_adjoint(
            frame_item[0], frame_item[1], frame_item[2], sensitivity, block
        ),
        (image_full, kspace, sampled),
    )
    grad_half = lax.psum_scatter(coil_partial, "coil", scatter_dimension=1, tiled=True).astype(
        jnp.bfloat16
    )
    grad_rows = lax.all_to_all(grad_half, "frame", split_axis=1, concat_axis=0, tiled=True)
    spatial_grad = factor_grad(temporal_all, grad_rows)
    temporal_part = lax.psum_scatter(
        frame_grad(spatial, grad_rows), "frame", scatter_dimension=0, tiled=True
    )
    temporal_grad = lax.psum(temporal_part, "coil")
    return (spatial_grad, temporal_grad)


def solution(mesh):
    placed = (
        P(("cuts", "coil", "frame"), None, None),
        P(("cuts", "frame"), None),
        P(("cuts", "frame"), "coil", None, None),
        P(("cuts", "frame"), None),
        P(("cuts", "coil"), None, None),
    )
    return jax.shard_map(
        on_device,
        mesh=mesh,
        in_specs=placed,
        out_specs=(P(("cuts", "coil", "frame"), None, None), P(("cuts", "frame"), None)),
        check_vma=False,
    )
```

profile of v0, /device:TPU:0, one launch (start us, length us, event | category | flops | bytes accessed | tf_op | source)
XLA Modules:
  0.0 152.4 jit_solution(3036720703098302424)
XLA Ops:
  0.6 22.5 %all-gather = bf16[8,2,64]{2,1,0:T(2,128)(2,1)S(1)} all-gather(bf16[1,2,64]{2,1,0:T(2,128)(2,1)} %bitcast.83), channel_id=1, replica_groups=mesh['cuts'=2,'frame'=8,'coil'=2] {'frame'}, dimensions={0}, use_global_device_ids=true | all-gather | bytes 2304 | tf_op jit(solution)/shard_map/all_gather | solution.py:89
  25.3 1.2 fusion.22
  26.5 1.2 fusion.23
  28.6 3.4 %all-to-all-start = ((bf16[16,16,512]{2,1,0:T(8,128)(2,1)}), bf16[16,16,512]{2,1,0:T(8,128)(2,1)S(1)}, u32[]{:S(2)}, u32[]{:S(2)}) async-start(bf16[16,16,512]{2,1,0:T(8,128)(2,1)} %copy.13), calls=%async_computation | async-start | bytes 524288 | tf_op jit(solution)/shard_map/all_to_all | solution.py:91
  32.0 1.3 dynamic-slice
  36.9 3.3 %all-to-all-done = bf16[16,16,512]{2,1,0:T(8,128)(2,1)S(1)} async-done(((bf16[16,16,512]{2,1,0:T(8,128)(2,1)}), bf16[16,16,512]{2,1,0:T(8,128)(2,1)S(1)}, u32[]{:S(2)}, u32[]{:S(2)}) %all-to-all-start) | async-done | bytes 262176 | tf_op jit(solution)/shard_map/all_to_all | solution.py:91
  40.2 2.2 %all_gather.7 = bf16[2,256,512]{2,1,0:T(8,128)(2,1)S(1)} all-gather(bf16[2,128,512]{2,1,0:T(8,128)(2,1)S(1)} %bitcast.70), channel_id=1, replica_groups=mesh['cuts'=2,'frame'=8,'coil'=2] {'coil'}, dimensions={1}, use_global_device_ids=true | all-gather | bytes 786432 | tf_op jit(solution)/shard_map/all_gather | solution.py:92
  42.4 62.9 %while.10 = (s32[]{:T(128)}, f32[2,256,512]{2,0,1:T(2,128)}, bf16[16,256,512]{2,1,0:T(8,128)(2,1)}, s32[2,256]{1,0:T(2,128)S(1)}, bf16[2,256,512]{2,1,0:T(8,128)...) while((s32[]{:T(128)}, f32[2,256,512]{2,0,1:T(2,128)}, ...), condition=%wide.region_3.4_spmd, body=%wide.region_0.3_spmd.sunk | while | flops 4330750976 | bytes 107749048 | solution.py:93
  42.5 3.4 %convert_element_type.64 = f32[16,256,512]{2,1,0:T(8,128)S(1)} convert(bf16[16,256,512]{2,1,0:T(8,128)(2,1)} %get-tuple-element.137) | non-fusion elementwise | flops 2097152 | bytes 12582912 | tf_op jit(solution)/shard_map/while/body/eval_jaxpr/convert_element_type | solution.py:64
  45.9 3.0 %subtract_convert_fusion.2 = (bf16[16,256,256]{2,1,0:T(8,128)(2,1)S(1)}, bf16[16,256,256]{2,1,0:T(8,128)(2,1)}) fusion(f32[16,256,512]{2,1,0:T(8,128)S(1)} %convert_element_type.64, f32[256,256]{1,0:T(8,128)S(1)} %get-tuple-element.111, f32[256,256]{1,0:T(8,128)S(1)} %get-tuple-element.112), kind=kLoop, calls=%fused_computation.13.clone.1 | loop fusion | flops 8388608 | bytes 13107200 | tf_op jit(solution)/shard_map/convert.2
  49.7 10.8 %fusion.65 = f32[16,256,512]{2,1,0:T(8,128)} fusion(bf16[2,16,256,512]{3,2,1,0:T(8,128)(2,1)} %get-tuple-element.141, s32[]{:T(128)} %get-tuple-element.126, f32[512]{0:T(512)S(1)} %add_convert_fusion.3, bf16[16,256,256]{2,1,0:T(8,128)(2,1)} %get-tuple-element.113, bf16[16,256,256]{2,1,0:T(8,128)(2,1)S(1)} %get-tuple-element.114, ...), kind=kOutput, calls=%fused_computation.3.clone.1 | convolution fusion | flops 4311744512 | bytes 17828352 | tf_op jit(solution)/shard_map/while/body/eval_jaxpr/dot_general | solution.py:76
  60.5 7.0 %add_reduce_fusion.2 = (f32[256,256]{1,0:T(8,128)S(1)}, f32[256,256]{1,0:T(8,128)S(1)}) fusion(f32[16,256,512]{2,1,0:T(8,128)} %fusion.65, f32[16,256,512]{2,1,0:T(8,128)} %copy-done), kind=kLoop, calls=%fused_computation.10.clone.1 | loop fusion | flops 8257536 | bytes 17301504 | tf_op jit(solution)/shard_map/while/body/eval_jaxpr/reduce_sum | solution.py:82
  68.2 4.7 %dynamic_update_slice.5 = f32[2,256,512]{2,0,1:T(2,128)S(1)} dynamic-update-slice(f32[2,256,512]{2,0,1:T(2,128)S(1)} %copy-done.2, f32[1,256,512]{2,0,1:T(1,128)S(1)} %copy.22, s32[]{:T(128)} %get-tuple-element.126, s32[]{:T(128)} %constant.31.clone.1..sunk, s32[]{:T(128)} %constant.31.clone.1..sunk) | dynamic-update-slice | bytes 1048580 | tf_op jit(solution)/shard_map/while/body/jit(dynamic_update_index_in_dim)/dynamic_update_slice | solution.py:93
  74.0 3.3 %convert_element_type.64 = f32[16,256,512]{2,1,0:T(8,128)S(1)} convert(bf16[16,256,512]{2,1,0:T(8,128)(2,1)} %get-tuple-element.137) | non-fusion elementwise | flops 2097152 | bytes 12582912 | tf_op jit(solution)/shard_map/while/body/eval_jaxpr/convert_element_type | solution.py:64
  77.3 3.0 %subtract_convert_fusion.2 = (bf16[16,256,256]{2,1,0:T(8,128)(2,1)S(1)}, bf16[16,256,256]{2,1,0:T(8,128)(2,1)}) fusion(f32[16,256,512]{2,1,0:T(8,128)S(1)} %convert_element_type.64, f32[256,256]{1,0:T(8,128)S(1)} %get-tuple-element.111, f32[256,256]{1,0:T(8,128)S(1)} %get-tuple-element.112), kind=kLoop, calls=%fused_computation.13.clone.1 | loop fusion | flops 8388608 | bytes 13107200 | tf_op jit(solution)/shard_map/convert.2
  81.2 10.8 %fusion.65 = f32[16,256,512]{2,1,0:T(8,128)} fusion(bf16[2,16,256,512]{3,2,1,0:T(8,128)(2,1)} %get-tuple-element.141, s32[]{:T(128)} %get-tuple-element.126, f32[512]{0:T(512)S(1)} %add_convert_fusion.3, bf16[16,256,256]{2,1,0:T(8,128)(2,1)} %get-tuple-element.113, bf16[16,256,256]{2,1,0:T(8,128)(2,1)S(1)} %get-tuple-element.114, ...), kind=kOutput, calls=%fused_computation.3.clone.1 | convolution fusion | flops 4311744512 | bytes 17828352 | tf_op jit(solution)/shard_map/while/body/eval_jaxpr/dot_general | solution.py:76
  91.9 7.0 %add_reduce_fusion.2 = (f32[256,256]{1,0:T(8,128)S(1)}, f32[256,256]{1,0:T(8,128)S(1)}) fusion(f32[16,256,512]{2,1,0:T(8,128)} %fusion.65, f32[16,256,512]{2,1,0:T(8,128)} %copy-done), kind=kLoop, calls=%fused_computation.10.clone.1 | loop fusion | flops 8257536 | bytes 17301504 | tf_op jit(solution)/shard_map/while/body/eval_jaxpr/reduce_sum | solution.py:82
  99.6 4.7 %dynamic_update_slice.5 = f32[2,256,512]{2,0,1:T(2,128)S(1)} dynamic-update-slice(f32[2,256,512]{2,0,1:T(2,128)S(1)} %copy-done.2, f32[1,256,512]{2,0,1:T(1,128)S(1)} %copy.22, s32[]{:T(128)} %get-tuple-element.126, s32[]{:T(128)} %constant.31.clone.1..sunk, s32[]{:T(128)} %constant.31.clone.1..sunk) | dynamic-update-slice | bytes 1048580 | tf_op jit(solution)/shard_map/while/body/jit(dynamic_update_index_in_dim)/dynamic_update_slice | solution.py:93
  105.3 6.9 %all-reduce.3 = bf16[2,256,512]{2,0,1:T(2,128)(2,1)S(1)} all-reduce(f32[2,256,512]{2,0,1:T(2,128)} %get-tuple-element.39), channel_id=2, replica_groups=mesh['cuts'=2,'frame'=8,'coil'=2] {'coil'}, use_global_device_ids=true, to_apply=%region_4.5.clone | all-reduce | flops 262144 | bytes 1572864
  113.1 3.4 %all-to-all-start.1 = ((bf16[2,128,512]{2,0,1:T(2,128)(2,1)}), bf16[2,128,512]{2,0,1:T(2,128)(2,1)S(1)}, u32[]{:S(2)}, u32[]{:S(2)}) async-start(bf16[2,128,512]{2,0,1:T(2,128)(2,1)} %dynamic-slice_convert_fusion), calls=%async_computation.1 | async-start | bytes 524288 | tf_op jit(solution)/shard_map/all_to_all | solution.py:102
  117.7 8.4 %all-to-all-done.1 = bf16[2,128,512]{2,0,1:T(2,128)(2,1)S(1)} async-done(((bf16[2,128,512]{2,0,1:T(2,128)(2,1)}), bf16[2,128,512]{2,0,1:T(2,128)(2,1)S(1)}, u32[]{:S(2)}, u32[]{:S(2)}) %all-to-all-start.1) | async-done | bytes 262176 | tf_op jit(solution)/shard_map/all_to_all | solution.py:102
  127.9 19.6 %all-reduce.1 = f32[16,64]{1,0:T(8,128)S(1)} all-reduce(f32[16,64]{1,0:T(8,128)S(1)} %pad_maximum_fusion.2), channel_id=3, replica_groups=mesh['cuts'=2,'frame'=8,'coil'=2] {'frame'}, use_global_device_ids=true, to_apply=%region_5.6.clone | all-reduce | flops 1024 | bytes 8192
  147.6 3.0 %psum.7 = f32[2,64]{1,0:T(2,128)} all-reduce(f32[2,64]{1,0:T(2,128)S(1)} %constant_dynamic-slice_fusion.1), channel_id=1, replica_groups=mesh['cuts'=2,'frame'=8,'coil'=2] {'coil'}, use_global_device_ids=true, to_apply=%region_6.7 | all-reduce | flops 128 | bytes 1024 | tf_op jit(solution)/shard_map/psum | solution.py:107
  151.3 1.1 pad_maximum_fusion
  (53 shorter events, 15.0 us)
Async XLA Ops:
  0.6 41.7 %copy-start.4 = (s32[2,256]{1,0:T(2,128)S(1)}, s32[2,256]{1,0:T(2,128)}, u32[]{:S(2)}) copy-start(s32[2,256]{1,0:T(2,128)} %param.10) | copy-start | bytes 6148
  28.6 11.6 %all-to-all-start = ((bf16[16,16,512]{2,1,0:T(8,128)(2,1)}), bf16[16,16,512]{2,1,0:T(8,128)(2,1)S(1)}, u32[]{:S(2)}, u32[]{:S(2)}) async-start(bf16[16,16,512]{2,1,0:T(8,128)(2,1)} %copy.13), calls=%async_computation | async-start | bytes 524288 | tf_op jit(solution)/shard_map/all_to_all | solution.py:91
  42.4 74.1 %copy-start.5 = (u32[32]{0:T(128)S(1)}, u32[32]{0:T(128)}, u32[]{:S(2)}) copy-start(u32[32]{0:T(128)} %constant.47) | copy-start | bytes 388
  42.4 84.1 %copy-start.1 = (bf16[16,32,512]{2,1,0:T(8,128)(2,1)S(1)}, bf16[16,32,512]{2,1,0:T(8,128)(2,1)}, u32[]{:S(2)}) copy-start(bf16[16,32,512]{2,1,0:T(8,128)(2,1)} %param.7) | copy-start | bytes 1572868
  45.9 3.8 %copy-start = (f32[16,256,512]{2,1,0:T(8,128)}, f32[16,256,512]{2,1,0:T(8,128)S(1)}, u32[]{:S(2)}) copy-start(f32[16,256,512]{2,1,0:T(8,128)S(1)} %convert_element_type.64) | copy-start | bytes 25165828 | tf_op jit(solution)/shard_map/while
  60.5 7.6 %copy-start.2 = (f32[2,256,512]{2,0,1:T(2,128)S(1)}, f32[2,256,512]{2,0,1:T(2,128)}, u32[]{:S(2)}) copy-start(f32[2,256,512]{2,0,1:T(2,128)} %get-tuple-element.127) | copy-start | bytes 3145732 | tf_op jit(solution)/shard_map/while
  72.9 1.0 copy-start.3
  77.3 3.8 %copy-start = (f32[16,256,512]{2,1,0:T(8,128)}, f32[16,256,512]{2,1,0:T(8,128)S(1)}, u32[]{:S(2)}) copy-start(f32[16,256,512]{2,1,0:T(8,128)S(1)} %convert_element_type.64) | copy-start | bytes 25165828 | tf_op jit(solution)/shard_map/while
  91.9 7.6 %copy-start.2 = (f32[2,256,512]{2,0,1:T(2,128)S(1)}, f32[2,256,512]{2,0,1:T(2,128)}, u32[]{:S(2)}) copy-start(f32[2,256,512]{2,0,1:T(2,128)} %get-tuple-element.127) | copy-start | bytes 3145732 | tf_op jit(solution)/shard_map/while
  104.3 1.0 copy-start.3
  113.1 13.1 %all-to-all-start.1 = ((bf16[2,128,512]{2,0,1:T(2,128)(2,1)}), bf16[2,128,512]{2,0,1:T(2,128)(2,1)S(1)}, u32[]{:S(2)}, u32[]{:S(2)}) async-start(bf16[2,128,512]{2,0,1:T(2,128)(2,1)} %dynamic-slice_convert_fusion), calls=%async_computation.1 | async-start | bytes 524288 | tf_op jit(solution)/shard_map/all_to_all | solution.py:102
where the time goes:
time: 153 us; the launch traced here: 152 us
  blocking collectives  54.2 us (35%)
  other arithmetic  31 us (20%)
  matrix products  28.1 us (18%)
  local copies, waits for them, and re-layouts  18.2 us (12%)
  waiting for transfers between devices  11.7 us (8%)
  starting transfers between devices  6.82 us (4%)
  between operations  2.1 us (1%)
    unnamed x2, blocking collectives  26.5 us
    all_gather x1, blocking collectives, on_device(): temporal_all = lax.all_gather(temporal, 'frame', axis=0, tiled=True)  22.5 us
    dot_general x2, matrix products, coil_adjoint(): jnp.dot(misfit.reshape(coil_count * row_count, full_width), block.T, pref...  21.6 us
    reduce_sum x2, other arithmetic, coil_adjoint(): grad_real = jnp.sum(sens_real * back_real + sens_imag * back_imag, axis=0)  14 us
    dynamic_update_slice x4, local copies, waits for them, and re-layouts, on_device(): lax.map(lambda frame_item: coil_adjoint(frame_item[0], frame_item[1], fra...  10.5 us
    all_to_all x1, waiting for transfers between devices, on_device(): lax.all_to_all(grad_half, 'frame', split_axis=1, concat_axis=0, tiled=True)  8.41 us
    another operation x4, other arithmetic  8 us
    convert_element_type x2, other arithmetic, coil_adjoint(): sens_real, sens_imag = split_parts(sensitivity.astype(jnp.float32))  6.72 us
  transfers between devices with their start and end apart: 2, of which 2 were waited for; matrix products, arithmetic and copies ran while one was open for 3% of the time, Pallas kernels for 0%

commit v1 on v0

--- a/solution.py
+++ b/solution.py
@@ -99,7 +99,12 @@
     grad_half = lax.psum_scatter(coil_partial, "coil", scatter_dimension=1, tiled=True).astype(
         jnp.bfloat16
     )
-    grad_rows = lax.all_to_all(grad_half, "frame", split_axis=1, concat_axis=0, tiled=True)
+    grad_rows = jnp.concatenate(
+        lax.all_to_all(
+            jnp.stack(jnp.split(grad_half, lax.axis_size("frame"), axis=1)), "frame", 0, 0
+        ),
+        axis=0,
+    )
     spatial_grad = factor_grad(temporal_all, grad_rows)
     temporal_part = lax.psum_scatter(
         frame_grad(spatial, grad_rows), "frame", scatter_dimension=0, tiled=True

time: 153 us -> 163 us (1.065)
  between operations: 2.1 us -> 14.8 us
  waiting for transfers between devices: 11.7 us -> 20 us
  local copies, waits for them, and re-layouts: 18.2 us -> 10.2 us
  blocking collectives: 54.2 us -> 47.3 us
  starting transfers between devices: 6.82 us -> 9.29 us
    dynamic_update_slice x4 -> x0, local copies, waits for them, and re-layouts: 10.5 us -> none  [on_device(): lax.map(lambda frame_item: coil_adjoint(frame_item[0], frame_item[1], fra...]
    unnamed x2 -> x1, blocking collectives: 26.5 us -> 19.7 us
    reduce_scatter x0 -> x1, waiting for transfers between devices: none -> 6.79 us  [on_device(): lax.psum_scatter(coil_partial, 'coil', scatter_dimension=1, tiled=True)]
    unnamed x9 -> x15, local copies, waits for them, and re-layouts: 1.88 us -> 4.93 us
    all_to_all x1, starting transfers between devices: 3.41 us -> 5.84 us  [on_device(): lax.all_to_all(jnp.stack(jnp.split(grad_half, lax.axis_size('frame'), axi...]
    all_to_all x1, waiting for transfers between devices: 3.29 us -> 5.16 us  [on_device(): lax.all_to_all(image_rows, 'frame', split_axis=0, concat_axis=1, tiled=True)]
  transfers between devices with their start and end apart: 2 -> 3, of which waited for: 2 -> 3; matrix products, arithmetic and copies ran while one was open for 3% -> 2% of each run, Pallas kernels for 0% -> 0%
where the time goes in v1:
time: 163 us; the launch traced here: 162 us
  blocking collectives  47.3 us (29%)
  other arithmetic  32.1 us (20%)
  matrix products  28.2 us (17%)
  waiting for transfers between devices  20 us (12%)
  between operations  14.8 us (9%)
  local copies, waits for them, and re-layouts  10.2 us (6%)
  starting transfers between devices  9.29 us (6%)
    all_gather x1, blocking collectives, on_device(): temporal_all = lax.all_gather(temporal, 'frame', axis=0, tiled=True)  22.5 us
    dot_general x2, matrix products, coil_adjoint(): jnp.dot(misfit.reshape(coil_count * row_count, full_width), block.T, pref...  21.6 us
    unnamed x1, blocking collectives  19.7 us
    reduce_sum x2, other arithmetic, coil_adjoint(): grad_real = jnp.sum(sens_real * back_real + sens_imag * back_imag, axis=0)  14 us
    all_to_all x1, waiting for transfers between devices, on_device(): lax.all_to_all(jnp.stack(jnp.split(grad_half, lax.axis_size('frame'), axi...  8.08 us
    another operation x4, other arithmetic  7.96 us
    reduce_scatter x1, waiting for transfers between devices, on_device(): lax.psum_scatter(coil_partial, 'coil', scatter_dimension=1, tiled=True)  6.79 us
    convert_element_type x2, other arithmetic, coil_adjoint(): sens_real, sens_imag = split_parts(sensitivity.astype(jnp.float32))  6.72 us
  transfers between devices with their start and end apart: 3, of which 3 were waited for; matrix products, arithmetic and copies ran while one was open for 2% of the time, Pallas kernels for 0%

profile of v1, /device:TPU:0, one launch (start us, length us, event | category | flops | bytes accessed | tf_op | source)
XLA Modules:
  0.0 162.1 jit_solution(7080085500894493702)
XLA Ops:
  7.2 22.5 %all-gather = bf16[8,2,64]{2,1,0:T(2,128)(2,1)S(1)} all-gather(bf16[1,2,64]{2,1,0:T(2,128)(2,1)} %bitcast.110), channel_id=1, replica_groups=mesh['cuts'=2,'frame'=8,'coil'=2] {'frame'}, dimensions={0}, use_global_device_ids=true | all-gather | bytes 2304 | tf_op jit(solution)/shard_map/all_gather | solution.py:89
  29.6 1.1 fusion.42
  30.8 1.1 fusion.36
  31.9 1.2 fusion.23
  33.1 1.2 fusion.24
  35.1 3.4 %all-to-all-start = ((bf16[16,16,512]{2,1,0:T(8,128)(2,1)}), bf16[16,16,512]{2,1,0:T(8,128)(2,1)S(1)}, u32[]{:S(2)}, u32[]{:S(2)}) async-start(bf16[16,16,512]{2,1,0:T(8,128)(2,1)} %copy.9), calls=%async_computation | async-start | bytes 524288 | tf_op jit(solution)/shard_map/all_to_all | solution.py:91
  39.6 1.1 negate_convert_fusion
  41.5 5.2 %all-to-all-done = bf16[16,16,512]{2,1,0:T(8,128)(2,1)S(1)} async-done(((bf16[16,16,512]{2,1,0:T(8,128)(2,1)}), bf16[16,16,512]{2,1,0:T(8,128)(2,1)S(1)}, u32[]{:S(2)}, u32[]{:S(2)}) %all-to-all-start) | async-done | bytes 262176 | tf_op jit(solution)/shard_map/all_to_all | solution.py:91
  46.7 2.2 %all_gather.7 = bf16[2,256,512]{2,1,0:T(8,128)(2,1)S(1)} all-gather(bf16[2,128,512]{2,1,0:T(8,128)(2,1)S(1)} %bitcast.98), channel_id=1, replica_groups=mesh['cuts'=2,'frame'=8,'coil'=2] {'coil'}, dimensions={1}, use_global_device_ids=true | all-gather | bytes 786432 | tf_op jit(solution)/shard_map/all_gather | solution.py:92
  48.9 52.4 %while.10 = (s32[]{:T(128)}, f32[2,256,512]{2,1,0:T(8,128)}, bf16[16,256,512]{2,1,0:T(8,128)(2,1)}, s32[2,256]{1,0:T(2,128)S(1)}, bf16[2,256,512]{2,1,0:T(8,128)...) while((s32[]{:T(128)}, f32[2,256,512]{2,1,0:T(8,128)}, ...), condition=%wide.region_3.4_spmd, body=%wide.region_0.3_spmd.sunk | while | flops 4330750976 | bytes 105651888 | solution.py:93
  49.0 3.4 %convert_element_type.63 = f32[16,256,512]{2,1,0:T(8,128)S(1)} convert(bf16[16,256,512]{2,1,0:T(8,128)(2,1)} %get-tuple-element.137) | non-fusion elementwise | flops 2097152 | bytes 12582912 | tf_op jit(solution)/shard_map/while/body/eval_jaxpr/convert_element_type | solution.py:64
  52.4 2.9 %subtract_convert_fusion.2 = (bf16[16,256,256]{2,1,0:T(8,128)(2,1)S(1)}, bf16[16,256,256]{2,1,0:T(8,128)(2,1)}) fusion(f32[16,256,512]{2,1,0:T(8,128)S(1)} %convert_element_type.63, f32[256,256]{1,0:T(8,128)S(1)} %get-tuple-element.113, f32[256,256]{1,0:T(8,128)S(1)} %get-tuple-element.114), kind=kLoop, calls=%fused_computation.13.clone.1 | loop fusion | flops 8388608 | bytes 13107200 | tf_op jit(solution)/shard_map/convert.2
  56.3 10.8 %fusion.76 = f32[16,256,512]{2,1,0:T(8,128)} fusion(bf16[2,16,256,512]{3,2,1,0:T(8,128)(2,1)} %get-tuple-element.141, s32[]{:T(128)} %get-tuple-element.127, f32[512]{0:T(512)S(1)} %add_convert_fusion.3, bf16[16,256,256]{2,1,0:T(8,128)(2,1)} %get-tuple-element.115, bf16[16,256,256]{2,1,0:T(8,128)(2,1)S(1)} %get-tuple-element.116, ...), kind=kOutput, calls=%fused_computation.3.clone.1 | convolution fusion | flops 4311744512 | bytes 17828352 | tf_op jit(solution)/shard_map/while/body/eval_jaxpr/dot_general | solution.py:76
  67.1 7.0 %add_reduce_fusion.2 = (f32[256,256]{1,0:T(8,128)S(1)}, f32[256,256]{1,0:T(8,128)S(1)}) fusion(f32[16,256,512]{2,1,0:T(8,128)} %fusion.76, f32[16,256,512]{2,1,0:T(8,128)} %copy-done), kind=kLoop, calls=%fused_computation.10.clone.1 | loop fusion | flops 8257536 | bytes 17301504 | tf_op jit(solution)/shard_map/while/body/eval_jaxpr/reduce_sum | solution.py:82
  75.2 3.3 %convert_element_type.63 = f32[16,256,512]{2,1,0:T(8,128)S(1)} convert(bf16[16,256,512]{2,1,0:T(8,128)(2,1)} %get-tuple-element.137) | non-fusion elementwise | flops 2097152 | bytes 12582912 | tf_op jit(solution)/shard_map/while/body/eval_jaxpr/convert_element_type | solution.py:64
  78.6 2.9 %subtract_convert_fusion.2 = (bf16[16,256,256]{2,1,0:T(8,128)(2,1)S(1)}, bf16[16,256,256]{2,1,0:T(8,128)(2,1)}) fusion(f32[16,256,512]{2,1,0:T(8,128)S(1)} %convert_element_type.63, f32[256,256]{1,0:T(8,128)S(1)} %get-tuple-element.113, f32[256,256]{1,0:T(8,128)S(1)} %get-tuple-element.114), kind=kLoop, calls=%fused_computation.13.clone.1 | loop fusion | flops 8388608 | bytes 13107200 | tf_op jit(solution)/shard_map/convert.2
  82.4 10.8 %fusion.76 = f32[16,256,512]{2,1,0:T(8,128)} fusion(bf16[2,16,256,512]{3,2,1,0:T(8,128)(2,1)} %get-tuple-element.141, s32[]{:T(128)} %get-tuple-element.127, f32[512]{0:T(512)S(1)} %add_convert_fusion.3, bf16[16,256,256]{2,1,0:T(8,128)(2,1)} %get-tuple-element.115, bf16[16,256,256]{2,1,0:T(8,128)(2,1)S(1)} %get-tuple-element.116, ...), kind=kOutput, calls=%fused_computation.3.clone.1 | convolution fusion | flops 4311744512 | bytes 17828352 | tf_op jit(solution)/shard_map/while/body/eval_jaxpr/dot_general | solution.py:76
  93.2 7.0 %add_reduce_fusion.2 = (f32[256,256]{1,0:T(8,128)S(1)}, f32[256,256]{1,0:T(8,128)S(1)}) fusion(f32[16,256,512]{2,1,0:T(8,128)} %fusion.76, f32[16,256,512]{2,1,0:T(8,128)} %copy-done), kind=kLoop, calls=%fused_computation.10.clone.1 | loop fusion | flops 8257536 | bytes 17301504 | tf_op jit(solution)/shard_map/while/body/eval_jaxpr/reduce_sum | solution.py:82
  101.3 6.8 %reduce-scatter.2.cloned.1.call-done = f32[2,128,512]{2,1,0:T(8,128)} async-done(((f32[2,256,512]{2,1,0:T(8,128)}), f32[2,128,512]{2,1,0:T(8,128)}) %reduce-scatter.2.cloned.1.call-update) | async-done | bytes 524304 | tf_op jit(solution)/shard_map/reduce_scatter | solution.py:99
  114.1 5.8 %all-to-all-start.1 = ((bf16[8,2,16,512]{3,2,1,0:T(8,128)(2,1)}), bf16[8,2,16,512]{3,2,1,0:T(8,128)(2,1)S(1)}, u32[]{:S(2)}, u32[]{:S(2)}) async-start(bf16[8,2,16,512]{3,2,1,0:T(8,128)(2,1)} %fusion.54), calls=%async_computation.2 | async-start | bytes 524288 | tf_op jit(solution)/shard_map/all_to_all | solution.py:103
  121.2 8.1 %all-to-all-done.1 = bf16[8,2,16,512]{3,2,1,0:T(8,128)(2,1)S(1)} async-done(((bf16[8,2,16,512]{3,2,1,0:T(8,128)(2,1)}), bf16[8,2,16,512]{3,2,1,0:T(8,128)(2,1)S(1)}, u32[]{:S(2)}, u32[]{:S(2)}) %all-to-all-start.1) | async-done | bytes 262176 | tf_op jit(solution)/shard_map/all_to_all | solution.py:103
  130.7 19.7 %all-reduce = f32[16,64]{1,0:T(8,128)S(1)} all-reduce(f32[16,64]{1,0:T(8,128)S(1)} %pad_maximum_fusion.2), channel_id=3, replica_groups=mesh['cuts'=2,'frame'=8,'coil'=2] {'frame'}, use_global_device_ids=true, to_apply=%region_5.6.clone | all-reduce | flops 1024 | bytes 8192
  150.4 3.0 %psum.7 = f32[2,64]{1,0:T(2,128)} all-reduce(f32[2,64]{1,0:T(2,128)S(1)} %constant_dynamic-slice_fusion.1), channel_id=1, replica_groups=mesh['cuts'=2,'frame'=8,'coil'=2] {'coil'}, use_global_device_ids=true, to_apply=%region_6.7 | all-reduce | flops 128 | bytes 1024 | tf_op jit(solution)/shard_map/psum | solution.py:112
  154.2 1.1 pad_maximum_fusion
  (57 shorter events, 15.5 us)
Async XLA Ops:
  7.2 41.7 %copy-start.4 = (s32[2,256]{1,0:T(2,128)S(1)}, s32[2,256]{1,0:T(2,128)}, u32[]{:S(2)}) copy-start(s32[2,256]{1,0:T(2,128)} %param.10) | copy-start | bytes 6148
  35.1 11.6 %all-to-all-start = ((bf16[16,16,512]{2,1,0:T(8,128)(2,1)}), bf16[16,16,512]{2,1,0:T(8,128)(2,1)S(1)}, u32[]{:S(2)}, u32[]{:S(2)}) async-start(bf16[16,16,512]{2,1,0:T(8,128)(2,1)} %copy.9), calls=%async_computation | async-start | bytes 524288 | tf_op jit(solution)/shard_map/all_to_all | solution.py:91
  38.5 69.6 %reduce-scatter.2.cloned.1.call-start = ((), (), s32[]{:S(2)}) async-start(), calls=%async_computation.3 | async-start | bytes 1572864 | tf_op jit(solution)/shard_map/reduce_scatter | solution.py:99
  48.9 71.1 %copy-start.5 = (u32[32]{0:T(128)S(1)}, u32[32]{0:T(128)}, u32[]{:S(2)}) copy-start(u32[32]{0:T(128)} %constant.43) | copy-start | bytes 388
  48.9 80.4 %copy-start.1 = (bf16[16,32,512]{2,1,0:T(8,128)(2,1)S(1)}, bf16[16,32,512]{2,1,0:T(8,128)(2,1)}, u32[]{:S(2)}) copy-start(bf16[16,32,512]{2,1,0:T(8,128)(2,1)} %param.7) | copy-start | bytes 1572868
  52.4 3.8 %copy-start = (f32[16,256,512]{2,1,0:T(8,128)}, f32[16,256,512]{2,1,0:T(8,128)S(1)}, u32[]{:S(2)}) copy-start(f32[16,256,512]{2,1,0:T(8,128)S(1)} %convert_element_type.63) | copy-start | bytes 25165828 | tf_op jit(solution)/shard_map/while
  67.1 7.0 %copy-start.2 = (f32[2,256,512]{2,1,0:T(8,128)S(1)}, f32[2,256,512]{2,1,0:T(8,128)}, u32[]{:S(2)}) copy-start(f32[2,256,512]{2,1,0:T(8,128)} %get-tuple-element.128) | copy-start | bytes 3145732 | tf_op jit(solution)/shard_map/while
  74.2 1.0 copy-start.3
  78.6 3.8 %copy-start = (f32[16,256,512]{2,1,0:T(8,128)}, f32[16,256,512]{2,1,0:T(8,128)S(1)}, u32[]{:S(2)}) copy-start(f32[16,256,512]{2,1,0:T(8,128)S(1)} %convert_element_type.63) | copy-start | bytes 25165828 | tf_op jit(solution)/shard_map/while
  93.2 7.0 %copy-start.2 = (f32[2,256,512]{2,1,0:T(8,128)S(1)}, f32[2,256,512]{2,1,0:T(8,128)}, u32[]{:S(2)}) copy-start(f32[2,256,512]{2,1,0:T(8,128)} %get-tuple-element.128) | copy-start | bytes 3145732 | tf_op jit(solution)/shard_map/while
  100.3 1.0 copy-start.3
  114.1 15.2 %all-to-all-start.1 = ((bf16[8,2,16,512]{3,2,1,0:T(8,128)(2,1)}), bf16[8,2,16,512]{3,2,1,0:T(8,128)(2,1)S(1)}, u32[]{:S(2)}, u32[]{:S(2)}) async-start(bf16[8,2,16,512]{3,2,1,0:T(8,128)(2,1)} %fusion.54), calls=%async_computation.2 | async-start | bytes 524288 | tf_op jit(solution)/shard_map/all_to_all | solution.py:103
Sparse Core Ops, SparseCore 0:
  101.5 6.6 reduce-scatter.1
